TPU v7x, 256 devices: a whole 4x4x8 slice. The times are simulated.
256 devices in a mesh: gx: 16 (over x, z_hi), gy: 16 (over z_lo, y, core).
Axes of the slice: x: 4, y: 4, z: 8 (z_hi: 4, z_lo: 2; z = z_hi * 2 + z_lo), core: 2. Of those that a mesh axis runs over, the one named last changes fastest.
Arguments:
- tokens: bfloat16 [256, 256, 2, 512], P('gx', 'gy'), may hold values from -6 to 6
- cotangent: bfloat16 [256, 256, 2, 512], P('gx', 'gy'), may hold values from -6 to 6
- gain_x: float32 [512], replicated, may hold values from 0.1 to 1.9
- w_qkv_x: bfloat16 [512, 1536], replicated, may hold values from -5 to 5, as said below
- w_out_x: bfloat16 [512, 512], replicated, may hold values from -0.25 to 0.25
- gain_y: float32 [512], replicated, may hold values from 0.1 to 1.9
- w_qkv_y: bfloat16 [512, 1536], replicated, may hold values from -5 to 5, as said below
- w_out_y: bfloat16 [512, 512], replicated, may hold values from -0.25 to 0.25
- gain_mlp: float32 [512], replicated, may hold values from 0.1 to 1.9
- w_up: bfloat16 [512, 2048], replicated, may hold values from -0.25 to 0.25
- w_down: bfloat16 [2048, 512], replicated, may hold values from -0.125 to 0.125
Outputs:
- grad_tokens: bfloat16 [256, 256, 2, 512], P('gx', 'gy')
Inputs may be any that keep to these rules, and one draw needn't show every extreme that they name: `w_qkv_x`: query, key and value projections side by side. `w_qkv_y`: query, key and value projections side by side.
All inputs are finite; a program needn't handle non-finite values.
Results may differ from a plain program's by a relative error of at most 0.013.
Values may be sent and summed in bfloat16 or wider, within the bound.
A program may use at most 128 MiB of HBM per device.

v0:
```python
from functools import partial
import jax
import jax.numpy as jnp
from jax import lax
from jax.sharding import PartitionSpec as P

D = 512
HEADS = 8


def to_low(tensor):
    return lax.optimization_barrier(tensor.astype(jnp.bfloat16))


def layer_norm(inputs, norm_gain):
    average = jnp.mean(inputs, -1, keepdims=True)
    centred = inputs - average
    variance = jnp.mean(centred * centred, -1, keepdims=True)
    return centred * lax.rsqrt(variance + 1e-05) * norm_gain


def norm_back(inputs, norm_gain, gradient):
    _, pullback = jax.vjp(lambda tensor: layer_norm(tensor, norm_gain), inputs)
    return pullback(gradient)[0]


def project(tensor, weight):
    lead_dims = tensor.shape[:-1]
    flattened = tensor.reshape(-1, tensor.shape[-1])
    result = jnp.dot(flattened, weight, preferred_element_type=jnp.float32)
    return result.reshape(lead_dims + (weight.shape[1],))


def project_back(tensor, weight):
    lead_dims = tensor.shape[:-1]
    flattened = tensor.reshape(-1, tensor.shape[-1])
    result = lax.dot_general(
        flattened, weight, (((1,), (1,)), ((), ())), preferred_element_type=jnp.float32
    )
    return result.reshape(lead_dims + (weight.shape[0],))


def to_xlines(tensor):
    return lax.all_to_all(tensor, "gx", split_axis=1, concat_axis=0, tiled=True)


def from_xlines(tensor):
    return lax.all_to_all(tensor, "gx", split_axis=0, concat_axis=1, tiled=True)


def to_ylines(tensor):
    return lax.all_to_all(tensor, "gy", split_axis=0, concat_axis=1, tiled=True)


def from_ylines(tensor):
    return lax.all_to_all(tensor, "gy", split_axis=1, concat_axis=0, tiled=True)


def heads_of(tensor, which_part):
    lead_dims = tensor.shape[:-1]
    block_part = tensor[..., which_part * D : (which_part + 1) * D]
    return block_part.reshape(lead_dims + (HEADS, D // HEADS))


def softmax_rows(queries, key_part, layout, key_layout):
    scores = jnp.einsum(
        layout + "hd," + key_layout + "hd->bzhqk",
        queries,
        key_part,
        preferred_element_type=jnp.float32,
    )
    scores = scores * (D // HEADS) ** (-0.5)
    highest = jnp.max(scores, -1, keepdims=True)
    exponent = jnp.exp(scores - highest)
    return exponent / jnp.sum(exponent, -1, keepdims=True)


def attend(qkv_proj, layout):
    key_layout = layout.replace("q", "k")
    queries, key_part, value_part = (
        heads_of(qkv_proj, 0),
        heads_of(qkv_proj, 1),
        heads_of(qkv_proj, 2),
    )
    probs_low = softmax_rows(queries, key_part, layout, key_layout).astype(jnp.bfloat16)
    result = jnp.einsum(
        "bzhqk," + key_layout + "hd->" + layout + "hd",
        probs_low,
        value_part,
        preferred_element_type=jnp.float32,
    )
    return result.reshape(qkv_proj.shape[:-1] + (D,)).astype(jnp.bfloat16)


def attend_back(qkv_proj, grad_out, layout):
    key_layout = layout.replace("q", "k")
    scale = (D // HEADS) ** (-0.5)
    queries, key_part, value_part = (
        heads_of(qkv_proj, 0),
        heads_of(qkv_proj, 1),
        heads_of(qkv_proj, 2),
    )
    probs = softmax_rows(queries, key_part, layout, key_layout)
    probs_low = probs.astype(jnp.bfloat16)
    grad_heads = heads_of(grad_out, 0)
    grad_probs = jnp.einsum(
        layout + "hd," + key_layout + "hd->bzhqk",
        grad_heads,
        value_part,
        preferred_element_type=jnp.float32,
    )
    grad_scores = probs * (grad_probs - jnp.sum(probs * grad_probs, -1, keepdims=True))
    grad_low = grad_scores.astype(jnp.bfloat16)
    grad_q = jnp.einsum(
        "bzhqk," + key_layout + "hd->" + layout + "hd",
        grad_low,
        key_part,
        preferred_element_type=jnp.float32,
    )
    grad_k = jnp.einsum(
        "bzhqk," + layout + "hd->" + key_layout + "hd",
        grad_low,
        queries,
        preferred_element_type=jnp.float32,
    )
    grad_v = jnp.einsum(
        "bzhqk," + layout + "hd->" + key_layout + "hd",
        probs_low,
        grad_heads,
        preferred_element_type=jnp.float32,
    )
    lead_dims = qkv_proj.shape[:-1] + (D,)
    return jnp.concatenate(
        [
            (grad_q * scale).astype(jnp.bfloat16).reshape(lead_dims),
            (grad_k * scale).astype(jnp.bfloat16).reshape(lead_dims),
            grad_v.astype(jnp.bfloat16).reshape(lead_dims),
        ],
        -1,
    )


def mix_lines(stream, norm_gain, w_qkv, w_out, layout):
    stream_f = stream.astype(jnp.float32)
    normed = layer_norm(stream_f, norm_gain).astype(jnp.bfloat16)
    qkv_lines = project(normed, w_qkv).astype(jnp.bfloat16)
    mixed_out = attend(qkv_lines, layout)
    updated = to_low(stream_f + project(mixed_out, w_out))
    return (updated, qkv_lines)


def back_lines(stream, gradient, qkv_lines, norm_gain, w_qkv, w_out, layout):
    grad_mixed = project_back(gradient, w_out).astype(jnp.bfloat16)
    grad_qkv = attend_back(qkv_lines, grad_mixed, layout)
    grad_normed = project_back(grad_qkv, w_qkv)
    return to_low(
        gradient.astype(jnp.float32) + norm_back(stream.astype(jnp.float32), norm_gain, grad_normed)
    )


def mlp_back(stream, cotangent, gain_mlp, w_up, w_down):
    stream_f = stream.astype(jnp.float32)
    normed = layer_norm(stream_f, gain_mlp).astype(jnp.bfloat16)
    pre_act = project(normed, w_up)
    grad_act = project_back(cotangent, w_down).astype(jnp.bfloat16)
    _, pullback = jax.vjp(partial(jax.nn.gelu, approximate=True), pre_act)
    grad_pre = pullback(grad_act.astype(jnp.float32))[0].astype(jnp.bfloat16)
    return to_low(
        cotangent.astype(jnp.float32) + norm_back(stream_f, gain_mlp, project_back(grad_pre, w_up))
    )


def local(
    tokens, cotangent, gain_x, w_qkv_x, w_out_x, gain_y, w_qkv_y, w_out_y, gain_mlp, w_up, w_down
):
    tokens_x = to_xlines(tokens)
    cotangent_y = to_ylines(cotangent)
    stream_1x, qkv_x = mix_lines(tokens_x, gain_x, w_qkv_x, w_out_x, "qbz")
    stream_1 = to_ylines(from_xlines(stream_1x))
    stream_2, qkv_y = mix_lines(stream_1, gain_y, w_qkv_y, w_out_y, "bqz")
    grad_2 = mlp_back(stream_2, cotangent_y, gain_mlp, w_up, w_down)
    grad_1y = back_lines(stream_1, grad_2, qkv_y, gain_y, w_qkv_y, w_out_y, "bqz")
    grad_1 = to_xlines(from_ylines(grad_1y))
    grad_x = back_lines(tokens_x, grad_1, qkv_x, gain_x, w_qkv_x, w_out_x, "qbz")
    return from_xlines(grad_x)


def solution(mesh):
    in_specs = (
        P("gx", "gy", None, None),
        P("gx", "gy", None, None),
        P(),
        P(),
        P(),
        P(),
        P(),
        P(),
        P(),
        P(),
        P(),
    )
    out_specs = P("gx", "gy", None, None)
    return jax.shard_map(local, mesh=mesh, in_specs=in_specs, out_specs=out_specs, check_vma=False)
```

profile of v0, /device:TPU:24, one launch (start us, length us, event | category | flops | bytes accessed | tf_op | source)
XLA Modules:
  0.0 229.5 jit_solution(3078606832670182966)
XLA Ops:
  0.0 1.7 copy.222
  1.7 29.5 %all_to_all.93 = bf16[16,16,2,512]{3,2,0,1:T(2,128)(2,1)S(1)} all-to-all(bf16[16,16,2,512]{3,2,0,1:T(2,128)(2,1)S(1)} %copy.222), channel_id=1, replica_groups=mesh['gx'=16,'gy'=16] {'gx'}, dimensions={1} | all-to-all | bytes 1048576 | tf_op jit(solution)/shard_map/all_to_all | solution.py:44
  34.0 2.4 %fusion.18 = bf16[256,1,2,1536]{3,0,2,1:T(8,128)(2,1)S(1)} fusion(bf16[512,1536]{1,0:T(8,128)(2,1)} %param.14, f32[256,2,512]{2,0,1:T(8,128)S(1)} %bitcast.211, f32[512]{0:T(512)S(1)} %copy-done.21, f32[256,2]{0,1:T(2,128)S(1)} %rsqrt.36, f32[256,2]{0,1:T(2,128)S(1)} %div.94), kind=kOutput, calls=%fused_computation.29 | convolution fusion | flops 807141376 | bytes 4200448 | tf_op jit(solution)/shard_map/dot_general | solution.py:30
  36.5 1.2 fusion.126
  37.7 2.1 copy.229
  39.8 2.1 copy.228
  41.8 2.0 copy.227
  43.9 4.6 %fusion.127 = (f32[2,8,256]{2,1,0:T(8,128)S(1)}, f32[2,8,256,256]{2,3,1,0:T(8,128)}) fusion(bf16[256,2,8,64]{0,3,2,1:T(8,128)(2,1)} %bitcast.225, bf16[256,2,8,64]{0,3,2,1:T(8,128)(2,1)} %bitcast.223), kind=kOutput, calls=%fused_computation.157 | convolution fusion | flops 137363712 | bytes 5259264 | tf_op jit(solution)/shard_map/sub | solution.py:74
  48.5 2.9 %convolution_convert_fusion.8 = bf16[2,8,64,256]{3,2,1,0:T(8,128)(2,1)S(1)} fusion(bf16[256,2,8,64]{0,3,2,1:T(8,128)(2,1)} %bitcast.237, f32[2,8,256,256]{2,3,1,0:T(8,128)} %get-tuple-element.12, f32[2,8,256]{2,1,0:T(8,128)S(1)} %get-tuple-element.11), kind=kOutput, calls=%fused_computation.79 | convolution fusion | flops 136577024 | bytes 5259264 | tf_op jit(solution)/shard_map/bzhqk,kbzhd->qbzhd/dot_general | solution.py:86
  52.5 21.3 %all_to_all.94 = bf16[256,1,2,512]{3,2,1,0:T(2,128)(2,1)} all-to-all(bf16[256,1,2,512]{3,2,1,0:T(2,128)(2,1)S(1)} %copy.232), channel_id=1, replica_groups=mesh['gx'=16,'gy'=16] {'gx'}, dimensions={0} | all-to-all | bytes 1048576 | tf_op jit(solution)/shard_map/all_to_all | solution.py:48
  73.7 4.7 %all-to-all-start = ((bf16[16,16,2,512]{3,2,1,0:T(2,128)(2,1)}), bf16[16,16,2,512]{3,2,1,0:T(2,128)(2,1)}, u32[]{:S(2)}, u32[]{:S(2)}) async-start(bf16[16,16,2,512]{3,2,1,0:T(2,128)(2,1)} %param.12), calls=%async_computation | async-start | bytes 1048576 | tf_op jit(solution)/shard_map/all_to_all | solution.py:52
  78.4 2.1 copy.285
  80.6 6.6 %all-to-all-done = bf16[16,16,2,512]{3,2,1,0:T(2,128)(2,1)} async-done(((bf16[16,16,2,512]{3,2,1,0:T(2,128)(2,1)}), bf16[16,16,2,512]{3,2,1,0:T(2,128)(2,1)}, u32[]{:S(2)}, u32[]{:S(2)}) %all-to-all-start) | async-done | bytes 524320 | tf_op jit(solution)/shard_map/all_to_all | solution.py:52
  87.1 6.3 %all-to-all-start.3 = ((bf16[16,16,2,512]{3,1,2,0:T(8,128)(2,1)}), bf16[16,16,2,512]{3,1,2,0:T(8,128)(2,1)}, u32[]{:S(2)}, u32[]{:S(2)}) async-start(bf16[16,16,2,512]{3,1,2,0:T(8,128)(2,1)} %bitcast.218), calls=%async_computation.3 | async-start | bytes 1048576 | tf_op jit(solution)/shard_map/all_to_all | solution.py:52
  93.5 1.1 copy.221
  94.6 2.2 copy.220
  96.8 2.7 %convolution_convert_fusion.2 = bf16[256,2,2048]{2,0,1:T(8,128)(2,1)} fusion(bf16[256,2,512]{2,0,1:T(8,128)(2,1)S(1)} %bitcast.247, bf16[2048,512]{1,0:T(8,128)(2,1)S(1)} %copy-done), kind=kOutput, calls=%fused_computation.28 | convolution fusion | flops 1074790400 | bytes 4718592 | tf_op jit(solution)/shard_map/dot_general | solution.py:37
  99.5 2.7 %all-to-all-done.3 = bf16[16,16,2,512]{3,1,2,0:T(8,128)(2,1)} async-done(((bf16[16,16,2,512]{3,1,2,0:T(8,128)(2,1)}), bf16[16,16,2,512]{3,1,2,0:T(8,128)(2,1)}, u32[]{:S(2)}, u32[]{:S(2)}) %all-to-all-start.3) | async-done | bytes 524320 | tf_op jit(solution)/shard_map/all_to_all | solution.py:52
  102.2 1.2 convert_reduce_fusion.1
  103.5 1.3 multiply_reduce_fusion.6
  104.9 1.2 copy.234
  106.3 2.4 %fusion.19 = bf16[1,256,2,1536]{3,1,2,0:T(8,128)(2,1)S(1)} fusion(bf16[256,2,512]{2,0,1:T(8,128)(2,1)S(1)} %multiply_convert_fusion.2, bf16[512,1536]{1,0:T(8,128)(2,1)} %param.17), kind=kOutput, calls=%fused_computation.30 | convolution fusion | flops 806092800 | bytes 3670016 | tf_op jit(solution)/shard_map/dot_general | solution.py:30
  108.7 1.1 fusion.125
  110.0 1.4 copy.241
  111.5 2.3 copy.240
  113.7 3.5 %fusion.128 = (f32[2,8,256]{2,1,0:T(8,128)S(1)}, f32[2,8,256,256]{2,3,1,0:T(8,128)}) fusion(bf16[256,2,8,64]{0,3,2,1:T(8,128)(2,1)S(1)} %bitcast.229, bf16[256,2,8,64]{0,3,2,1:T(8,128)(2,1)S(1)} %bitcast.227), kind=kOutput, calls=%fused_computation.158 | convolution fusion | flops 137363712 | bytes 5259264 | tf_op jit(solution)/shard_map/sub | solution.py:74
  117.2 2.9 %convolution_convert_fusion.7 = bf16[2,8,64,256]{3,2,1,0:T(8,128)(2,1)S(1)} fusion(bf16[256,2,8,64]{0,3,2,1:T(8,128)(2,1)} %bitcast.239, f32[2,8,256,256]{2,3,1,0:T(8,128)} %get-tuple-element.14, f32[2,8,256]{2,1,0:T(8,128)S(1)} %get-tuple-element.13), kind=kOutput, calls=%fused_computation.78 | convolution fusion | flops 136577024 | bytes 5259264 | tf_op jit(solution)/shard_map/bzhqk,bkzhd->bqzhd/dot_general | solution.py:86
  121.1 7.9 %fusion.80 = (f32[256,2]{0,1:T(2,128)S(1)}, f32[256,2,512]{2,0,1:T(8,128)}) fusion(bf16[1,256,2,512]{3,1,2,0:T(8,128)(2,1)S(1)} %fusion.75, f32[256,2]{0,1:T(2,128)S(1)} %broadcast_multiply_fusion.1, f32[512]{0:T(512)S(1)} %copy-done.20, bf16[512,2048]{1,0:T(8,128)(2,1)} %param.20, bf16[256,2,2048]{2,0,1:T(8,128)(2,1)} %convolution_convert_fusion.2, ...), kind=kOutput, calls=%fused_computation.91 | convolution fusion | flops 2172124672 | bytes 5775360 | tf_op jit(solution)/shard_map/dot_general | solution.py:37
  129.0 1.7 fusion.106
  130.7 1.9 fusion.82
  134.2 4.1 %convolution_convert_fusion.6 = bf16[2,8,64,256]{3,2,1,0:T(8,128)(2,1)} fusion(bf16[256,2,8,64]{0,3,2,1:T(8,128)(2,1)} %bitcast.243, f32[2,8,256,256]{2,3,1,0:T(8,128)} %get-tuple-element.14, f32[2,8,256]{2,1,0:T(8,128)S(1)} %get-tuple-element.13), kind=kOutput, calls=%fused_computation.77 | convolution fusion | flops 136577024 | bytes 5259264 | tf_op jit(solution)/shard_map/bzhqk,bqzhd->bkzhd/dot_general | solution.py:126
  140.5 1.6 fusion.70
  142.1 1.3 fusion.69
  143.4 1.3 copy.251
  144.6 2.0 copy.249
  146.7 2.0 copy.250
  148.7 2.8 %multiply_reduce_fusion.5 = (f32[256,2]{0,1:T(2,128)S(1)}, f32[256,2,512]{2,0,1:T(8,128)S(1)}) fusion(f32[16,16,2,512]{3,1,0,2:T(8,128)S(1)} %copy.234, f32[256,2]{0,1:T(2,128)S(1)} %div.99, f32[512]{0:T(512)S(1)} %copy-done.19, bf16[512,1536]{1,0:T(8,128)(2,1)} %param.17, bf16[256,2,512]{2,0,1:T(8,128)(2,1)S(1)} %copy.251, ...), kind=kOutput, calls=%fused_computation.100 | convolution fusion | flops 811073024 | bytes 5249024 | tf_op jit(solution)/shard_map/dot_general | solution.py:37
  152.9 13.5 %all_to_all.95 = bf16[1,256,2,512]{3,2,0,1:T(2,128)(2,1)S(1)} all-to-all(bf16[1,256,2,512]{3,2,0,1:T(2,128)(2,1)S(1)} %copy.252), channel_id=1, replica_groups=mesh['gx'=16,'gy'=16] {'gy'}, dimensions={1} | all-to-all | bytes 1048576 | tf_op jit(solution)/shard_map/all_to_all | solution.py:56
  166.7 22.4 %all_to_all.96 = bf16[16,16,2,512]{3,0,2,1:T(8,128)(2,1)S(1)} all-to-all(bf16[16,16,2,512]{3,0,2,1:T(8,128)(2,1)S(1)} %copy.253), channel_id=1, replica_groups=mesh['gx'=16,'gy'=16] {'gx'}, dimensions={1} | all-to-all | bytes 1048576 | tf_op jit(solution)/shard_map/all_to_all | solution.py:44
  190.6 3.9 %convolution_convert_fusion.5 = bf16[2,8,64,256]{3,2,1,0:T(8,128)(2,1)} fusion(bf16[256,2,8,64]{0,3,2,1:T(8,128)(2,1)S(1)} %bitcast.245, f32[2,8,256,256]{2,3,1,0:T(8,128)} %get-tuple-element.12, f32[2,8,256]{2,1,0:T(8,128)S(1)} %get-tuple-element.11), kind=kOutput, calls=%fused_computation.76 | convolution fusion | flops 136577024 | bytes 5259264 | tf_op jit(solution)/shard_map/bzhqk,qbzhd->kbzhd/dot_general | solution.py:126
  196.4 1.6 fusion.72
  198.0 1.3 fusion.71
  199.3 1.3 copy.261
  200.5 1.3 copy.259
  201.8 1.3 copy.260
  203.0 2.6 %multiply_reduce_fusion.4 = (f32[256,2]{0,1:T(2,128)S(1)}, f32[256,2,512]{2,0,1:T(8,128)S(1)}) fusion(f32[256,2,512]{2,0,1:T(8,128)S(1)} %bitcast.213, f32[256,2]{0,1:T(2,128)S(1)} %div.94, f32[512]{0:T(512)S(1)} %copy-done.21, bf16[512,1536]{1,0:T(8,128)(2,1)} %param.14, bf16[256,2,512]{2,0,1:T(8,128)(2,1)S(1)} %copy.261, ...), kind=kOutput, calls=%fused_computation.99 | convolution fusion | flops 811073024 | bytes 5249024 | tf_op jit(solution)/shard_map/dot_general | solution.py:37
  207.0 21.2 %all_to_all.97 = bf16[256,1,2,512]{3,2,1,0:T(2,128)(2,1)S(1)} all-to-all(bf16[256,1,2,512]{3,2,1,0:T(2,128)(2,1)S(1)} %copy.262), channel_id=1, replica_groups=mesh['gx'=16,'gy'=16] {'gx'}, dimensions={0} | all-to-all | bytes 1048576 | tf_op jit(solution)/shard_map/all_to_all | solution.py:48
  228.2 1.3 copy.284
  (93 shorter events, 15.5 us)
Async XLA Ops:
  0.0 96.8 %copy-start = (bf16[2048,512]{1,0:T(8,128)(2,1)S(1)}, bf16[2048,512]{1,0:T(8,128)(2,1)}, u32[]{:S(2)}) copy-start(bf16[2048,512]{1,0:T(8,128)(2,1)} %param.21) | copy-start | bytes 6291460
  0.0 34.0 %copy-start.21 = (f32[512]{0:T(512)S(1)}, f32[512]{0:T(512)}, u32[]{:S(2)}) copy-start(f32[512]{0:T(512)} %param.13) | copy-start | bytes 6148
  48.5 2.9 %copy-start.8 = (bf16[512,512]{1,0:T(8,128)(2,1)S(1)}, bf16[512,512]{1,0:T(8,128)(2,1)}, u32[]{:S(2)}) copy-start(bf16[512,512]{1,0:T(8,128)(2,1)} %param.15) | copy-start | bytes 1572868
  73.7 13.4 %all-to-all-start = ((bf16[16,16,2,512]{3,2,1,0:T(2,128)(2,1)}), bf16[16,16,2,512]{3,2,1,0:T(2,128)(2,1)}, u32[]{:S(2)}, u32[]{:S(2)}) async-start(bf16[16,16,2,512]{3,2,1,0:T(2,128)(2,1)} %param.12), calls=%async_computation | async-start | bytes 1048576 | tf_op jit(solution)/shard_map/all_to_all | solution.py:52
  87.1 15.1 %all-to-all-start.3 = ((bf16[16,16,2,512]{3,1,2,0:T(8,128)(2,1)}), bf16[16,16,2,512]{3,1,2,0:T(8,128)(2,1)}, u32[]{:S(2)}, u32[]{:S(2)}) async-start(bf16[16,16,2,512]{3,1,2,0:T(8,128)(2,1)} %bitcast.218), calls=%async_computation.3 | async-start | bytes 1048576 | tf_op jit(solution)/shard_map/all_to_all | solution.py:52
  96.8 9.3 %copy-start.19 = (f32[512]{0:T(512)S(1)}, f32[512]{0:T(512)}, u32[]{:S(2)}) copy-start(f32[512]{0:T(512)} %param.16) | copy-start | bytes 6148
  110.0 7.2 %copy-start.12 = (bf16[1,256,2,512]{1,3,2,0:T(8,128)(2,1)}, bf16[1,256,2,512]{1,3,2,0:T(8,128)(2,1)S(1)}, u32[]{:S(2)}) copy-start(bf16[1,256,2,512]{1,3,2,0:T(8,128)(2,1)S(1)} %copy.242) | copy-start | bytes 1572868
  111.5 8.7 %copy-start.14 = (bf16[1,256,2,512]{1,3,2,0:T(8,128)(2,1)}, bf16[1,256,2,512]{1,3,2,0:T(8,128)(2,1)S(1)}, u32[]{:S(2)}) copy-start(bf16[1,256,2,512]{1,3,2,0:T(8,128)(2,1)S(1)} %copy.241) | copy-start | bytes 1572868
  117.2 2.9 %copy-start.6 = (bf16[512,512]{1,0:T(8,128)(2,1)S(1)}, bf16[512,512]{1,0:T(8,128)(2,1)}, u32[]{:S(2)}) copy-start(bf16[512,512]{1,0:T(8,128)(2,1)} %param.18) | copy-start | bytes 1572868
  117.2 3.9 %copy-start.20 = (f32[512]{0:T(512)S(1)}, f32[512]{0:T(512)}, u32[]{:S(2)}) copy-start(f32[512]{0:T(512)} %param.19) | copy-start | bytes 6148
  129.0 3.7 %copy-start.7 = (bf16[512,512]{1,0:T(8,128)(2,1)S(1)}, bf16[512,512]{1,0:T(8,128)(2,1)}, u32[]{:S(2)}) copy-start(bf16[512,512]{1,0:T(8,128)(2,1)} %param.18) | copy-start | bytes 1572868
  134.2 4.1 %copy-start.5 = (f32[2,8,256,256]{2,3,1,0:T(8,128)S(1)}, f32[2,8,256,256]{2,3,1,0:T(8,128)}, u32[]{:S(2)}) copy-start(f32[2,8,256,256]{2,3,1,0:T(8,128)} %get-tuple-element.14) | copy-start | bytes 12582916
  134.2 4.1 %copy-start.17 = (bf16[1,256,2,512]{1,3,2,0:T(8,128)(2,1)S(1)}, bf16[1,256,2,512]{1,3,2,0:T(8,128)(2,1)}, u32[]{:S(2)}) copy-start(bf16[1,256,2,512]{1,3,2,0:T(8,128)(2,1)} %copy.240) | copy-start | bytes 1572868
  134.2 4.1 %copy-start.18 = (bf16[256,2,512]{0,2,1:T(8,128)(2,1)S(1)}, bf16[256,2,512]{0,2,1:T(8,128)(2,1)}, u32[]{:S(2)}) copy-start(bf16[256,2,512]{0,2,1:T(8,128)(2,1)} %copy.245) | copy-start | bytes 1572868
  139.4 1.0 copy-start.15
  139.4 2.7 %copy-start.13 = (bf16[1,256,2,512]{1,3,2,0:T(8,128)(2,1)S(1)}, bf16[1,256,2,512]{1,3,2,0:T(8,128)(2,1)}, u32[]{:S(2)}) copy-start(bf16[1,256,2,512]{1,3,2,0:T(8,128)(2,1)} %copy-done.12) | copy-start | bytes 1572868
  152.0 37.9 %copy-start.9 = (bf16[512,512]{1,0:T(8,128)(2,1)S(1)}, bf16[512,512]{1,0:T(8,128)(2,1)}, u32[]{:S(2)}) copy-start(bf16[512,512]{1,0:T(8,128)(2,1)} %param.15) | copy-start | bytes 1572868
  189.1 0.8 copy-start.2
  190.6 3.9 %copy-start.4 = (f32[2,8,256,256]{2,3,1,0:T(8,128)S(1)}, f32[2,8,256,256]{2,3,1,0:T(8,128)}, u32[]{:S(2)}) copy-start(f32[2,8,256,256]{2,3,1,0:T(8,128)} %get-tuple-element.12) | copy-start | bytes 12582916
  190.6 3.9 %copy-start.16 = (bf16[256,1,2,512]{0,3,2,1:T(8,128)(2,1)S(1)}, bf16[256,1,2,512]{0,3,2,1:T(8,128)(2,1)}, u32[]{:S(2)}) copy-start(bf16[256,1,2,512]{0,3,2,1:T(8,128)(2,1)} %copy.227) | copy-start | bytes 1572868
  195.4 1.0 copy-start.11
  195.4 2.6 %copy-start.10 = (bf16[256,1,2,512]{0,3,2,1:T(8,128)(2,1)S(1)}, bf16[256,1,2,512]{0,3,2,1:T(8,128)(2,1)}, u32[]{:S(2)}) copy-start(bf16[256,1,2,512]{0,3,2,1:T(8,128)(2,1)} %copy.229) | copy-start | bytes 1572868
  203.0 3.0 %copy-start.3 = (bf16[16,16,1,2,512]{4,1,0,3,2:T(8,128)(2,1)S(1)}, bf16[16,16,1,2,512]{4,1,0,3,2:T(8,128)(2,1)}, u32[]{:S(2)}) copy-start(bf16[16,16,1,2,512]{4,1,0,3,2:T(8,128)(2,1)} %copy-done.2) | copy-start | bytes 1572868
  205.6 23.9 %copy-start.1 = (bf16[2048,512]{1,0:T(8,128)(2,1)S(1)}, bf16[2048,512]{1,0:T(8,128)(2,1)}, u32[]{:S(2)}) copy-start(bf16[2048,512]{1,0:T(8,128)(2,1)} %param.21) | copy-start | bytes 6291460
where the time goes:
time: 231 us; the launch traced here: 229 us
  blocking collectives  108 us (47%)
  matrix products  52.3 us (23%)
  local copies, waits for them, and re-layouts  36.4 us (16%)
  other arithmetic  12.2 us (5%)
  starting transfers between devices  11 us (5%)
  waiting for transfers between devices  9.24 us (4%)
    all_to_all x2, blocking collectives, to_xlines(): return lax.all_to_all(tensor, 'gx', split_axis=1, concat_axis=0, tiled=True)  51.8 us
    all_to_all x2, blocking collectives, from_xlines(): return lax.all_to_all(tensor, 'gx', split_axis=0, concat_axis=1, tiled=True)  42.5 us
    dot_general x6, matrix products, project_back(): lax.dot_general(flattened, weight, (((1,), (1,)), ((), ())), preferred_el...  17 us
    all_to_all x1, blocking collectives, from_ylines(): return lax.all_to_all(tensor, 'gy', split_axis=1, concat_axis=0, tiled=True)  13.5 us
    slice x8, local copies, waits for them, and re-layouts, heads_of(): block_part = tensor[..., which_part * D:(which_part + 1) * D]  12.4 us
    all_to_all x2, starting transfers between devices, to_ylines(): return lax.all_to_all(tensor, 'gy', split_axis=0, concat_axis=1, tiled=True)  11 us
    all_to_all x2, waiting for transfers between devices, to_ylines(): return lax.all_to_all(tensor, 'gy', split_axis=0, concat_axis=1, tiled=True)  9.24 us
    concatenate x6, local copies, waits for them, and re-layouts, attend_back(): jnp.concatenate([(grad_q * scale).astype(jnp.bfloat16).reshape(lead_dims)...  9.1 us
  transfers between devices with their start and end apart: 2, of which 2 were waited for; matrix products, arithmetic and copies ran while one was open for 4% of the time, Pallas kernels for 0%

commit v1 on v0

--- a/solution.py
+++ b/solution.py
@@ -45,7 +45,10 @@
 
 
 def from_xlines(tensor):
-    return lax.all_to_all(tensor, "gx", split_axis=0, concat_axis=1, tiled=True)
+    return jnp.concatenate(
+        lax.all_to_all(jnp.stack(jnp.split(tensor, lax.axis_size("gx"), axis=0)), "gx", 0, 0),
+        axis=1,
+    )
 
 
 def to_ylines(tensor):

time: 231 us -> 214 us (0.926)
  local copies, waits for them, and re-layouts: 36.4 us -> 23 us
  other arithmetic: 12.2 us -> 8.71 us
  waiting for transfers between devices: 9.24 us -> 11.9 us
    slice x8, local copies, waits for them, and re-layouts: 12.4 us -> 8.03 us  [heads_of(): block_part = tensor[..., which_part * D:(which_part + 1) * D]]
    all_to_all x2 -> x0, local copies, waits for them, and re-layouts: 3.42 us -> none  [from_xlines(): return lax.all_to_all(tensor, 'gx', split_axis=0, concat_axis=1, tiled=True)]
    concatenate x6, local copies, waits for them, and re-layouts: 9.1 us -> 5.99 us  [attend_back(): jnp.concatenate([(grad_q * scale).astype(jnp.bfloat16).reshape(lead_dims)...]
    reshape x0 -> x2, local copies, waits for them, and re-layouts: none -> 2.7 us  [from_xlines(): jnp.concatenate(lax.all_to_all(jnp.stack(jnp.split(tensor, lax.axis_size(...]
    all_to_all x2, waiting for transfers between devices: 9.24 us -> 11.9 us  [to_ylines(): return lax.all_to_all(tensor, 'gy', split_axis=0, concat_axis=1, tiled=True)]
  transfers between devices with their start and end apart: 2 -> 2, of which waited for: 2 -> 2; matrix products, arithmetic and copies ran while one was open for 4% -> 2% of each run, Pallas kernels for 0% -> 0%
where the time goes in v1:
time: 214 us; the launch traced here: 213 us
  blocking collectives  108 us (50%)
  matrix products  50 us (23%)
  local copies, waits for them, and re-layouts  23 us (11%)
  waiting for transfers between devices  11.9 us (6%)
  starting transfers between devices  10.4 us (5%)
  other arithmetic  8.71 us (4%)
    all_to_all x2, blocking collectives, to_xlines(): return lax.all_to_all(tensor, 'gx', split_axis=1, concat_axis=0, tiled=True)  51.9 us
    all_to_all x2, blocking collectives, from_xlines(): lax.all_to_all(jnp.stack(jnp.split(tensor, lax.axis_size('gx'), axis=0)),...  42.4 us
    dot_general x6, matrix products, project_back(): lax.dot_general(flattened, weight, (((1,), (1,)), ((), ())), preferred_el...  17.1 us
    all_to_all x1, blocking collectives, from_ylines(): return lax.all_to_all(tensor, 'gy', split_axis=1, concat_axis=0, tiled=True)  13.5 us
    all_to_all x2, waiting for transfers between devices, to_ylines(): return lax.all_to_all(tensor, 'gy', split_axis=0, concat_axis=1, tiled=True)  11.9 us
    all_to_all x2, starting transfers between devices, to_ylines(): return lax.all_to_all(tensor, 'gy', split_axis=0, concat_axis=1, tiled=True)  10.4 us
    sub x2, matrix products, softmax_rows(): exponent = jnp.exp(scores - highest)  8.14 us
    slice x8, local copies, waits for them, and re-layouts, heads_of(): block_part = tensor[..., which_part * D:(which_part + 1) * D]  8.03 us
  transfers between devices with their start and end apart: 2, of which 2 were waited for; matrix products, arithmetic and copies ran while one was open for 2% of the time, Pallas kernels for 0%

profile of v1, /device:TPU:24, one launch (start us, length us, event | category | flops | bytes accessed | tf_op | source)
XLA Modules:
  0.0 212.6 jit_solution(18235330908141287686)
XLA Ops:
  0.0 1.7 copy.173
  1.7 29.5 %all_to_all.67 = bf16[16,16,2,512]{3,2,0,1:T(2,128)(2,1)S(1)} all-to-all(bf16[16,16,2,512]{3,2,0,1:T(2,128)(2,1)S(1)} %copy.173), channel_id=1, replica_groups=mesh['gx'=16,'gy'=16] {'gx'}, dimensions={1} | all-to-all | bytes 1048576 | tf_op jit(solution)/shard_map/all_to_all | solution.py:44
  32.1 2.8 %fusion.18 = bf16[256,1,2,1536]{3,0,2,1:T(8,128)(2,1)S(1)} fusion(bf16[512,1536]{1,0:T(8,128)(2,1)} %param.14, f32[256,2,512]{2,0,1:T(8,128)S(1)} %bitcast.332, f32[512]{0:T(512)S(1)} %copy-done.23, f32[256,2]{0,1:T(2,128)S(1)} %rsqrt.36, f32[256,2]{0,1:T(2,128)S(1)} %div.94), kind=kOutput, calls=%fused_computation.29 | convolution fusion | flops 807141376 | bytes 4200448 | tf_op jit(solution)/shard_map/dot_general | solution.py:30
  34.9 1.2 fusion.126
  36.1 2.0 copy.183
  38.2 2.0 copy.182
  40.2 2.0 copy.181
  42.2 4.6 %fusion.127 = (f32[2,8,256]{2,1,0:T(8,128)S(1)}, f32[2,8,256,256]{2,3,1,0:T(8,128)}) fusion(bf16[256,2,8,64]{0,3,2,1:T(8,128)(2,1)} %bitcast.346, bf16[256,2,8,64]{0,3,2,1:T(8,128)(2,1)} %bitcast.344), kind=kOutput, calls=%fused_computation.220 | convolution fusion | flops 137363712 | bytes 5259264 | tf_op jit(solution)/shard_map/sub | solution.py:77
  46.9 2.9 %convolution_convert_fusion.8 = bf16[2,8,64,256]{3,2,1,0:T(8,128)(2,1)S(1)} fusion(bf16[256,2,8,64]{0,3,2,1:T(8,128)(2,1)} %bitcast.358, f32[2,8,256,256]{2,3,1,0:T(8,128)} %get-tuple-element.12, f32[2,8,256]{2,1,0:T(8,128)S(1)} %get-tuple-element.11), kind=kOutput, calls=%fused_computation.79 | convolution fusion | flops 136577024 | bytes 5259264 | tf_op jit(solution)/shard_map/bzhqk,kbzhd->qbzhd/dot_general | solution.py:89
  50.5 21.2 %all_to_all.68 = bf16[16,16,1,2,512]{4,1,3,2,0:T(8,128)(2,1)S(1)} all-to-all(bf16[16,16,1,2,512]{4,1,3,2,0:T(8,128)(2,1)S(1)} %constant_dynamic-update-slice_fusion), channel_id=1, replica_groups=mesh['gx'=16,'gy'=16] {'gx'}, dimensions={0} | all-to-all | bytes 1048576 | tf_op jit(solution)/shard_map/all_to_all | solution.py:49
  71.6 4.7 %all-to-all-start = ((bf16[16,16,2,512]{3,2,1,0:T(2,128)(2,1)}), bf16[16,16,2,512]{3,2,1,0:T(2,128)(2,1)S(1)}, u32[]{:S(2)}, u32[]{:S(2)}) async-start(bf16[16,16,2,512]{3,2,1,0:T(2,128)(2,1)} %param.12), calls=%async_computation | async-start | bytes 1048576 | tf_op jit(solution)/shard_map/all_to_all | solution.py:55
  76.4 1.4 copy.186
  77.7 7.2 %all-to-all-done = bf16[16,16,2,512]{3,2,1,0:T(2,128)(2,1)S(1)} async-done(((bf16[16,16,2,512]{3,2,1,0:T(2,128)(2,1)}), bf16[16,16,2,512]{3,2,1,0:T(2,128)(2,1)S(1)}, u32[]{:S(2)}, u32[]{:S(2)}) %all-to-all-start) | async-done | bytes 524320 | tf_op jit(solution)/shard_map/all_to_all | solution.py:55
  84.9 5.7 %all-to-all-start.3 = ((bf16[16,16,2,512]{3,2,1,0:T(2,128)(2,1)}), bf16[16,16,2,512]{3,2,1,0:T(2,128)(2,1)S(1)}, u32[]{:S(2)}, u32[]{:S(2)}) async-start(bf16[16,16,2,512]{3,2,1,0:T(2,128)(2,1)} %copy.186), calls=%async_computation.3 | async-start | bytes 1048576 | tf_op jit(solution)/shard_map/all_to_all | solution.py:55
  90.8 1.1 copy.171
  91.9 2.7 %convolution_convert_fusion.2 = bf16[256,2,2048]{2,0,1:T(8,128)(2,1)} fusion(bf16[256,2,512]{2,0,1:T(8,128)(2,1)S(1)} %bitcast.368, bf16[2048,512]{1,0:T(8,128)(2,1)S(1)} %copy-done), kind=kOutput, calls=%fused_computation.28 | convolution fusion | flops 1074790400 | bytes 4718592 | tf_op jit(solution)/shard_map/dot_general | solution.py:37
  94.6 4.7 %all-to-all-done.3 = bf16[16,16,2,512]{3,2,1,0:T(2,128)(2,1)S(1)} async-done(((bf16[16,16,2,512]{3,2,1,0:T(2,128)(2,1)}), bf16[16,16,2,512]{3,2,1,0:T(2,128)(2,1)S(1)}, u32[]{:S(2)}, u32[]{:S(2)}) %all-to-all-start.3) | async-done | bytes 524320 | tf_op jit(solution)/shard_map/all_to_all | solution.py:55
  100.2 2.4 %fusion.19 = bf16[1,256,2,1536]{3,1,2,0:T(8,128)(2,1)S(1)} fusion(bf16[256,2,512]{2,0,1:T(8,128)(2,1)S(1)} %multiply_convert_fusion.2, bf16[512,1536]{1,0:T(8,128)(2,1)} %param.17), kind=kOutput, calls=%fused_computation.30 | convolution fusion | flops 806092800 | bytes 3670016 | tf_op jit(solution)/shard_map/dot_general | solution.py:30
  103.4 3.5 %fusion.128 = (f32[2,8,256]{2,1,0:T(8,128)S(1)}, f32[2,8,256,256]{2,3,1,0:T(8,128)}) fusion(bf16[256,2,8,64]{0,3,2,1:T(8,128)(2,1)S(1)} %bitcast.350, bf16[256,2,8,64]{0,3,2,1:T(8,128)(2,1)S(1)} %bitcast.348), kind=kOutput, calls=%fused_computation.221 | convolution fusion | flops 137363712 | bytes 5259264 | tf_op jit(solution)/shard_map/sub | solution.py:77
  106.9 2.7 %convolution_convert_fusion.7 = bf16[2,8,64,256]{3,2,1,0:T(8,128)(2,1)S(1)} fusion(bf16[256,2,8,64]{0,3,2,1:T(8,128)(2,1)S(1)} %bitcast.360, f32[2,8,256,256]{2,3,1,0:T(8,128)} %get-tuple-element.14, f32[2,8,256]{2,1,0:T(8,128)S(1)} %get-tuple-element.13), kind=kOutput, calls=%fused_computation.78 | convolution fusion | flops 136577024 | bytes 5259264 | tf_op jit(solution)/shard_map/bzhqk,bkzhd->bqzhd/dot_general | solution.py:89
  109.8 0.5 fusion.75
  110.7 8.0 %fusion.80 = (f32[256,2]{0,1:T(2,128)S(1)}, f32[256,2,512]{2,0,1:T(8,128)}) fusion(bf16[1,256,2,512]{3,1,2,0:T(8,128)(2,1)S(1)} %fusion.75, f32[256,2]{0,1:T(2,128)S(1)} %broadcast_multiply_fusion.1, f32[512]{0:T(512)S(1)} %copy-done.22, bf16[512,2048]{1,0:T(8,128)(2,1)} %param.20, bf16[256,2,2048]{2,0,1:T(8,128)(2,1)} %convolution_convert_fusion.2, ...), kind=kOutput, calls=%fused_computation.91 | convolution fusion | flops 2172124672 | bytes 5775360 | tf_op jit(solution)/shard_map/dot_general | solution.py:37
  118.8 1.7 fusion.106
  120.5 1.7 fusion.82
  122.2 0.5 convolution_convert_fusion.4
  122.9 3.1 %convolution_convert_fusion.6 = bf16[2,8,64,256]{3,2,1,0:T(8,128)(2,1)S(1)} fusion(bf16[256,2,8,64]{0,3,2,1:T(8,128)(2,1)S(1)} %bitcast.364, f32[2,8,256,256]{2,3,1,0:T(8,128)} %get-tuple-element.14, f32[2,8,256]{2,1,0:T(8,128)S(1)} %get-tuple-element.13), kind=kOutput, calls=%fused_computation.77 | convolution fusion | flops 136577024 | bytes 5259264 | tf_op jit(solution)/shard_map/bzhqk,bqzhd->bkzhd/dot_general | solution.py:129
  126.4 1.1 multiply_reduce_fusion.1
  127.5 0.9 multiply_convert_fusion.1
  128.5 0.8 fusion.70
  129.3 0.5 fusion.69
  129.8 1.0 copy.203
  131.0 1.0 copy.202
  132.0 2.8 %multiply_reduce_fusion.5 = (f32[256,2]{0,1:T(2,128)S(1)}, f32[256,2,512]{2,0,1:T(8,128)S(1)}) fusion(f32[256,2]{0,1:T(2,128)S(1)} %div.99, bf16[16,16,2,512]{3,2,1,0:T(2,128)(2,1)S(1)} %all-to-all-done.3, f32[512]{0:T(512)S(1)} %copy-done.21, bf16[512,1536]{1,0:T(8,128)(2,1)} %param.17, bf16[256,2,512]{2,0,1:T(8,128)(2,1)} %copy.203, ...), kind=kOutput, calls=%fused_computation.100 | convolution fusion | flops 811335168 | bytes 4724736 | tf_op jit(solution)/shard_map/dot_general | solution.py:37
  135.7 0.5 copy.204
  136.3 13.5 %all_to_all.69 = bf16[1,256,2,512]{3,2,0,1:T(2,128)(2,1)S(1)} all-to-all(bf16[1,256,2,512]{3,2,0,1:T(2,128)(2,1)S(1)} %copy.204), channel_id=1, replica_groups=mesh['gx'=16,'gy'=16] {'gy'}, dimensions={1} | all-to-all | bytes 1048576 | tf_op jit(solution)/shard_map/all_to_all | solution.py:59
  150.0 22.5 %all_to_all.70 = bf16[16,16,2,512]{3,0,2,1:T(8,128)(2,1)S(1)} all-to-all(bf16[16,16,2,512]{3,0,2,1:T(8,128)(2,1)S(1)} %copy.205), channel_id=1, replica_groups=mesh['gx'=16,'gy'=16] {'gx'}, dimensions={1} | all-to-all | bytes 1048576 | tf_op jit(solution)/shard_map/all_to_all | solution.py:44
  172.6 0.8 copy-done.4
  174.1 3.9 %convolution_convert_fusion.5 = bf16[2,8,64,256]{3,2,1,0:T(8,128)(2,1)} fusion(bf16[256,2,8,64]{0,3,2,1:T(8,128)(2,1)S(1)} %bitcast.366, f32[2,8,256,256]{2,3,1,0:T(8,128)} %get-tuple-element.12, f32[2,8,256]{2,1,0:T(8,128)S(1)} %get-tuple-element.11), kind=kOutput, calls=%fused_computation.76 | convolution fusion | flops 136577024 | bytes 5259264 | tf_op jit(solution)/shard_map/bzhqk,qbzhd->kbzhd/dot_general | solution.py:129
  178.0 0.8 multiply_reduce_fusion
  178.8 0.9 multiply_convert_fusion
  179.9 1.6 fusion.72
  181.4 1.3 fusion.71
  182.7 1.3 copy.213
  183.9 1.3 copy.211
  185.2 1.3 copy.212
  186.5 2.6 %multiply_reduce_fusion.4 = (f32[256,2]{0,1:T(2,128)S(1)}, f32[256,2,512]{2,0,1:T(8,128)S(1)}) fusion(f32[256,2,512]{2,0,1:T(8,128)S(1)} %bitcast.334, f32[256,2]{0,1:T(2,128)S(1)} %div.94, f32[512]{0:T(512)S(1)} %copy-done.23, bf16[512,1536]{1,0:T(8,128)(2,1)} %param.14, bf16[256,2,512]{2,0,1:T(8,128)(2,1)S(1)} %copy.213, ...), kind=kOutput, calls=%fused_computation.99 | convolution fusion | flops 811073024 | bytes 5249024 | tf_op jit(solution)/shard_map/dot_general | solution.py:37
  190.1 21.2 %all_to_all.71 = bf16[16,16,1,2,512]{4,1,3,2,0:T(8,128)(2,1)S(1)} all-to-all(bf16[16,16,1,2,512]{4,1,3,2,0:T(8,128)(2,1)S(1)} %constant_dynamic-update-slice_fusion.16), channel_id=1, replica_groups=mesh['gx'=16,'gy'=16] {'gx'}, dimensions={0} | all-to-all | bytes 1048576 | tf_op jit(solution)/shard_map/all_to_all | solution.py:49
  211.3 1.3 copy.214
  (124 shorter events, 7.6 us)
Async XLA Ops:
  0.0 91.9 %copy-start = (bf16[2048,512]{1,0:T(8,128)(2,1)S(1)}, bf16[2048,512]{1,0:T(8,128)(2,1)}, u32[]{:S(2)}) copy-start(bf16[2048,512]{1,0:T(8,128)(2,1)} %param.21) | copy-start | bytes 6291460
  0.0 32.1 %copy-start.23 = (f32[512]{0:T(512)S(1)}, f32[512]{0:T(512)}, u32[]{:S(2)}) copy-start(f32[512]{0:T(512)} %param.13) | copy-start | bytes 6148
  32.1 17.7 %copy-start.2 = (f32[16,16,1,2,512]{4,1,0,3,2:T(8,128)}, f32[16,16,1,2,512]{4,1,0,3,2:T(8,128)S(1)}, u32[]{:S(2)}) copy-start(f32[16,16,1,2,512]{4,1,0,3,2:T(8,128)S(1)} %copy.175) | copy-start | bytes 3145732
  46.9 2.9 %copy-start.10 = (bf16[512,512]{1,0:T(8,128)(2,1)S(1)}, bf16[512,512]{1,0:T(8,128)(2,1)}, u32[]{:S(2)}) copy-start(bf16[512,512]{1,0:T(8,128)(2,1)} %param.15) | copy-start | bytes 1572868
  71.6 13.3 %all-to-all-start = ((bf16[16,16,2,512]{3,2,1,0:T(2,128)(2,1)}), bf16[16,16,2,512]{3,2,1,0:T(2,128)(2,1)S(1)}, u32[]{:S(2)}, u32[]{:S(2)}) async-start(bf16[16,16,2,512]{3,2,1,0:T(2,128)(2,1)} %param.12), calls=%async_computation | async-start | bytes 1048576 | tf_op jit(solution)/shard_map/all_to_all | solution.py:55
  84.9 14.3 %all-to-all-start.3 = ((bf16[16,16,2,512]{3,2,1,0:T(2,128)(2,1)}), bf16[16,16,2,512]{3,2,1,0:T(2,128)(2,1)S(1)}, u32[]{:S(2)}, u32[]{:S(2)}) async-start(bf16[16,16,2,512]{3,2,1,0:T(2,128)(2,1)} %copy.186), calls=%async_computation.3 | async-start | bytes 1048576 | tf_op jit(solution)/shard_map/all_to_all | solution.py:55
  90.8 9.2 %copy-start.21 = (f32[512]{0:T(512)S(1)}, f32[512]{0:T(512)}, u32[]{:S(2)}) copy-start(f32[512]{0:T(512)} %param.16) | copy-start | bytes 6148
  102.9 6.7 %copy-start.14 = (bf16[1,256,2,512]{1,3,2,0:T(8,128)(2,1)}, bf16[1,256,2,512]{1,3,2,0:T(8,128)(2,1)S(1)}, u32[]{:S(2)}) copy-start(bf16[1,256,2,512]{1,3,2,0:T(8,128)(2,1)S(1)} %copy.194) | copy-start | bytes 1572868
  103.1 6.5 %copy-start.16 = (bf16[1,256,2,512]{1,3,2,0:T(8,128)(2,1)}, bf16[1,256,2,512]{1,3,2,0:T(8,128)(2,1)S(1)}, u32[]{:S(2)}) copy-start(bf16[1,256,2,512]{1,3,2,0:T(8,128)(2,1)S(1)} %copy.193) | copy-start | bytes 1572868
  103.3 3.5 %copy-start.19 = (bf16[1,256,2,512]{1,3,2,0:T(8,128)(2,1)}, bf16[1,256,2,512]{1,3,2,0:T(8,128)(2,1)S(1)}, u32[]{:S(2)}) copy-start(bf16[1,256,2,512]{1,3,2,0:T(8,128)(2,1)S(1)} %copy.192) | copy-start | bytes 1572868
  106.9 2.9 %copy-start.9 = (bf16[512,512]{1,0:T(8,128)(2,1)S(1)}, bf16[512,512]{1,0:T(8,128)(2,1)}, u32[]{:S(2)}) copy-start(bf16[512,512]{1,0:T(8,128)(2,1)} %param.18) | copy-start | bytes 1572868
  109.6 1.1 copy-start.22
  110.7 9.7 %copy-start.6 = (f32[16,16,2,512]{3,1,0,2:T(8,128)S(1)}, f32[16,16,2,512]{3,1,0,2:T(8,128)}, u32[]{:S(2)}) copy-start(f32[16,16,2,512]{3,1,0,2:T(8,128)} %copy.171) | copy-start | bytes 3145732
  122.8 3.5 %copy-start.8 = (f32[2,8,256,256]{2,3,1,0:T(8,128)S(1)}, f32[2,8,256,256]{2,3,1,0:T(8,128)}, u32[]{:S(2)}) copy-start(f32[2,8,256,256]{2,3,1,0:T(8,128)} %get-tuple-element.14) | copy-start | bytes 12582916
  122.8 3.6 %copy-start.20 = (bf16[1,256,2,512]{1,3,2,0:T(8,128)(2,1)S(1)}, bf16[1,256,2,512]{1,3,2,0:T(8,128)(2,1)}, u32[]{:S(2)}) copy-start(bf16[1,256,2,512]{1,3,2,0:T(8,128)(2,1)} %copy-done.19) | copy-start | bytes 1572868
  127.5 1.0 copy-start.17
  127.5 1.8 copy-start.15
  135.3 38.0 %copy-start.11 = (bf16[512,512]{1,0:T(8,128)(2,1)S(1)}, bf16[512,512]{1,0:T(8,128)(2,1)}, u32[]{:S(2)}) copy-start(bf16[512,512]{1,0:T(8,128)(2,1)} %param.15) | copy-start | bytes 1572868
  172.6 0.8 copy-start.4
  174.0 3.9 %copy-start.7 = (f32[2,8,256,256]{2,3,1,0:T(8,128)S(1)}, f32[2,8,256,256]{2,3,1,0:T(8,128)}, u32[]{:S(2)}) copy-start(f32[2,8,256,256]{2,3,1,0:T(8,128)} %get-tuple-element.12) | copy-start | bytes 12582916
  174.0 3.9 %copy-start.18 = (bf16[256,1,2,512]{0,3,2,1:T(8,128)(2,1)S(1)}, bf16[256,1,2,512]{0,3,2,1:T(8,128)(2,1)}, u32[]{:S(2)}) copy-start(bf16[256,1,2,512]{0,3,2,1:T(8,128)(2,1)} %copy.181) | copy-start | bytes 1572868
  178.8 1.0 copy-start.13
  178.8 2.6 %copy-start.12 = (bf16[256,1,2,512]{0,3,2,1:T(8,128)(2,1)S(1)}, bf16[256,1,2,512]{0,3,2,1:T(8,128)(2,1)}, u32[]{:S(2)}) copy-start(bf16[256,1,2,512]{0,3,2,1:T(8,128)(2,1)} %copy.183) | copy-start | bytes 1572868
  179.9 6.6 %copy-start.3 = (f32[16,16,1,2,512]{4,1,0,3,2:T(8,128)S(1)}, f32[16,16,1,2,512]{4,1,0,3,2:T(8,128)}, u32[]{:S(2)}) copy-start(f32[16,16,1,2,512]{4,1,0,3,2:T(8,128)} %copy-done.2) | copy-start | bytes 3145732
  186.5 3.0 %copy-start.5 = (bf16[16,16,1,2,512]{4,1,0,3,2:T(8,128)(2,1)S(1)}, bf16[16,16,1,2,512]{4,1,0,3,2:T(8,128)(2,1)}, u32[]{:S(2)}) copy-start(bf16[16,16,1,2,512]{4,1,0,3,2:T(8,128)(2,1)} %copy-done.4) | copy-start | bytes 1572868
  189.1 23.6 %copy-start.1 = (bf16[2048,512]{1,0:T(8,128)(2,1)S(1)}, bf16[2048,512]{1,0:T(8,128)(2,1)}, u32[]{:S(2)}) copy-start(bf16[2048,512]{1,0:T(8,128)(2,1)} %param.21) | copy-start | bytes 6291460
